TPU v7x, 256 devices: a whole 4x4x8 slice. The times are simulated.
256 devices in a mesh: seq: 16 (over z_lo, x), layer: 16 (over z_hi, y, core).
Axes of the slice: x: 4, y: 4, z: 8 (z_hi: 2, z_lo: 4; z = z_hi * 4 + z_lo), core: 2. Of those that a mesh axis runs over, the one named last changes fastest.
Arguments:
- train_inputs: bfloat16 [16, 2048, 4096], P('layer', 'seq'), may hold values from -6 to 6
- out_grads: bfloat16 [16, 2048, 14336], P('layer', 'seq'), may hold values from -6 to 6
- query_blocks: bfloat16 [16, 14336, 4096], P('layer', 'seq'), may hold values from -0.00018310547 to 0.00018310547
- basis_in: bfloat16 [16, 32, 128, 128], P('layer'), may hold values from -0.5 to 0.5
- basis_out: bfloat16 [16, 112, 128, 128], P('layer', 'seq'), may hold values from -0.5 to 0.5
- block_of: int32 [16, 16], P('layer'), may hold values from 0 to 15, each once within a row
Outputs:
- scores: float32 [2048], P('seq')
Inputs may be any that keep to these rules, and one draw needn't show every extreme that they name: Each row of block_of names every eigenbasis block of its layer once.
All inputs are finite; a program needn't handle non-finite values.
Results may differ from a plain program's by a relative error of at most 0.0055.
Values may be sent and summed in bfloat16 or wider, within the bound.
A program may use at most 128 MiB of HBM per device.

v0:
```python
import functools

import jax
import jax.numpy as jnp
from jax import lax
from jax.experimental import pallas as pl
from jax.experimental.pallas import tpu as pltpu
from jax.sharding import PartitionSpec as P

MESH = pl.DeviceIdType.MESH


def turn_rows(rows, basis):
    count = rows.shape[0]
    groups = rows.reshape(count, basis.shape[0], basis.shape[1])
    turned = jnp.einsum("tnr,nrs->tns", groups, basis, preferred_element_type=jnp.float32)
    return turned.reshape(count, -1).astype(jnp.bfloat16)


def reduce_kernel(ns, nl, part_ref, out_ref, slots1, mine, slots2, ssem1, rsem1, ssem2, rsem2):
    ms = lax.axis_index("seq")
    ml = lax.axis_index("layer")
    barrier = pltpu.get_barrier_semaphore()
    for d in range(1, ns):
        pl.semaphore_signal(barrier, inc=1, device_id=(lax.rem(ms + d, ns), ml), device_id_type=MESH)
    for d in range(1, nl):
        pl.semaphore_signal(barrier, inc=1, device_id=(ms, lax.rem(ml + d, nl)), device_id_type=MESH)
    pl.semaphore_wait(barrier, (ns - 1) + (nl - 1))

    sends = []
    for d in range(1, ns):
        j = lax.rem(ms + d, ns)
        c = pltpu.make_async_remote_copy(
            src_ref=part_ref.at[j], dst_ref=slots1.at[ms], send_sem=ssem1.at[j], recv_sem=rsem1.at[ms],
            device_id=(j, ml), device_id_type=MESH)
        c.start()
        sends.append(c)
    slots1[ms] = part_ref[ms]
    for d in range(1, ns):
        i = lax.rem(ms + ns - d, ns)
        pltpu.make_async_remote_copy(
            src_ref=part_ref.at[i], dst_ref=slots1.at[i], send_sem=ssem1.at[i], recv_sem=rsem1.at[i],
            device_id=(i, ml), device_id_type=MESH).wait_recv()
    for c in sends:
        c.wait_send()
    acc = slots1[0]
    for i in range(1, ns):
        acc = acc + slots1[i]
    mine[...] = acc

    sends = []
    for d in range(1, nl):
        j = lax.rem(ml + d, nl)
        c = pltpu.make_async_remote_copy(
            src_ref=mine, dst_ref=slots2.at[ml], send_sem=ssem2.at[j], recv_sem=rsem2.at[ml],
            device_id=(ms, j), device_id_type=MESH)
        c.start()
        sends.append(c)
    slots2[ml] = acc
    for d in range(1, nl):
        i = lax.rem(ml + nl - d, nl)
        pltpu.make_async_remote_copy(
            src_ref=mine, dst_ref=slots2.at[i], send_sem=ssem2.at[i], recv_sem=rsem2.at[i],
            device_id=(ms, i), device_id_type=MESH).wait_recv()
    for c in sends:
        c.wait_send()
    tot = slots2[0]
    for i in range(1, nl):
        tot = tot + slots2[i]
    out_ref[...] = tot


def comm_kernel(nx, nz, r1, x_ref, g_ref, xo_ref, go_ref, ssem, rsem, gssem, grsem, lsem):
    ns = nx * nz
    t = x_ref.shape[0]
    s = lax.axis_index("seq")
    lay = lax.axis_index("layer")
    zl = s // nx
    xx = lax.rem(s, nx)
    ha, hb = r1 // 2, (t - r1) // 2
    halves = ((pl.ds(0, ha), pl.ds(ha, ha)), (pl.ds(r1, hb), pl.ds(r1 + hb, hb)))
    whole = (pl.ds(0, r1), pl.ds(r1, t - r1))
    offsets = [e for k in range(1, nz) for e in (k, -k)]

    def on_line(e):
        return jnp.logical_and(zl + e >= 0, zl + e < nz)

    def at(e, dx):
        row = jnp.clip(zl + e, 0, nz - 1)
        return row * nx + lax.rem(xx + dx + nx, nx)

    barrier = pltpu.get_barrier_semaphore()
    for d in range(1, ns):
        pl.semaphore_signal(barrier, inc=1, device_id=(lax.rem(s + d, ns), lay), device_id_type=MESH)
    pl.semaphore_wait(barrier, ns - 1)

    own_x = pltpu.make_async_copy(x_ref, xo_ref.at[s], lsem.at[0])
    own_g = pltpu.make_async_copy(g_ref.at[s], go_ref.at[s], lsem.at[1])
    own_x.start()
    own_g.start()

    sends = []

    def rows(part, half):
        return whole[part] if half is None else halves[part][half]

    def sem(slot, part, half):
        return rsem.at[slot * 4 + part * 2 + (0 if half is None else half)]

    def guarded(cond, fn):
        if cond is None:
            fn()
        else:
            pl.when(cond)(fn)

    def send(e, dx, part, half, to, cond=None):
        slot = at(e, dx)
        rr = rows(part, half)
        src = x_ref.at[rr] if (e, dx) == (0, 0) else xo_ref.at[slot, rr]
        c = pltpu.make_async_remote_copy(
            src_ref=src, dst_ref=xo_ref.at[slot, rr], send_sem=ssem.at[len(sends)],
            recv_sem=sem(slot, part, half), device_id=(to, lay), device_id_type=MESH)
        guarded(cond, c.start)
        sends.append((c, cond))

    def recv(e, dx, part, half, cond=None):
        slot = at(e, dx)
        rr = rows(part, half)
        c = pltpu.make_async_remote_copy(
            src_ref=x_ref.at[rr], dst_ref=xo_ref.at[slot, rr], send_sem=ssem.at[0],
            recv_sem=sem(slot, part, half), device_id=(slot, lay), device_id_type=MESH)
        guarded(cond, c.wait_recv)

    right, left = at(0, 1), at(0, -1)
    for e in offsets:
        send(0, 0, 1, None, at(e, 0), on_line(e))
    for h in range(2):
        send(0, 0, 1, h, right)
        send(0, 0, 1, h, left)
    if r1:
        for h in range(2):
            send(0, 0, 0, h, right)
            send(0, 0, 0, h, left)
        for e in offsets:
            send(0, 0, 0, None, at(e, 0), on_line(e))
    gsends = []
    for d in range(1, ns):
        j = lax.rem(s + d, ns)
        c = pltpu.make_async_remote_copy(
            src_ref=g_ref.at[j], dst_ref=go_ref.at[s], send_sem=gssem.at[d - 1],
            recv_sem=grsem.at[s], device_id=(j, lay), device_id_type=MESH)
        c.start()
        gsends.append(c)
    for e in offsets:
        cond = on_line(e)
        recv(e, 0, 1, None, cond)
        for h in range(2):
            send(e, 0, 1, h, right, cond)
            send(e, 0, 1, h, left, cond)
    if r1:
        recv(0, -1, 0, 0)
        send(0, -1, 0, 0, right)
        recv(0, 1, 0, 1)
        send(0, 1, 0, 1, left)
        recv(0, -1, 0, 1)
        recv(0, 1, 0, 0)
        for e in offsets:
            for dx in (-1, 1):
                send(0, dx, 0, None, at(e, 0), on_line(e))
        recv(0, 2, 0, 0)
        recv(0, 2, 0, 1)
        for e in offsets:
            send(0, 2, 0, None, at(e, 0), on_line(e))
    for e, cond in [(0, None)] + [(e, on_line(e)) for e in offsets]:
        recv(e, -1, 1, 0, cond)
        send(e, -1, 1, 0, right, cond)
        recv(e, 1, 1, 1, cond)
        send(e, 1, 1, 1, left, cond)
    if r1:
        for e in offsets:
            for dx in range(nx):
                recv(e, dx, 0, None, on_line(e))
    for e, cond in [(0, None)] + [(e, on_line(e)) for e in offsets]:
        recv(e, -1, 1, 1, cond)
        recv(e, 1, 1, 0, cond)
        recv(e, 2, 1, 0, cond)
        recv(e, 2, 1, 1, cond)
    for d in range(1, ns):
        i = lax.rem(s + ns - d, ns)
        pltpu.make_async_remote_copy(
            src_ref=g_ref.at[i], dst_ref=go_ref.at[i], send_sem=gssem.at[d - 1],
            recv_sem=grsem.at[i], device_id=(i, lay), device_id_type=MESH).wait_recv()
    for c, cond in sends:
        guarded(cond, c.wait_send)
    for c in gsends:
        c.wait_send()
    own_x.wait()
    own_g.wait()


def exchange(rotated, outgoing, ns):
    nx = 4
    nz = ns // nx
    t, dim = rotated.shape
    w = outgoing.shape[-1]
    r1 = t // 8
    n_sends = 128
    return pl.pallas_call(
        functools.partial(comm_kernel, nx, nz, r1),
        out_shape=(jax.ShapeDtypeStruct((ns, t, dim), rotated.dtype), jax.ShapeDtypeStruct((ns, t, w), outgoing.dtype)),
        in_specs=[pl.BlockSpec(memory_space=pl.ANY)] * 2,
        out_specs=(pl.BlockSpec(memory_space=pl.ANY), pl.BlockSpec(memory_space=pl.ANY)),
        scratch_shapes=[
            pltpu.SemaphoreType.DMA((n_sends,)),
            pltpu.SemaphoreType.DMA((4 * ns,)),
            pltpu.SemaphoreType.DMA((ns - 1,)),
            pltpu.SemaphoreType.DMA((ns,)),
            pltpu.SemaphoreType.DMA((2,)),
        ],
        compiler_params=pltpu.CompilerParams(collective_id=1, has_side_effects=True),
    )(rotated, outgoing)


def pick_kernel(owners_ref, *refs):
    o_ref = refs[-1]
    for i, g_ref in enumerate(refs[:-1]):
        o_ref[i] = g_ref[...]


def pick_blocks(grads, owners, per_step=4):
    count, total = grads.shape
    nblk = owners.shape[0]
    width = total // nblk

    def spec(i):
        return pl.BlockSpec((count, width), lambda k, own: (0, own[k * per_step + i]))

    return pl.pallas_call(
        pick_kernel,
        out_shape=jax.ShapeDtypeStruct((nblk, count, width), grads.dtype),
        grid_spec=pltpu.PrefetchScalarGridSpec(
            num_scalar_prefetch=1,
            grid=(nblk // per_step,),
            in_specs=[spec(i) for i in range(per_step)],
            out_specs=pl.BlockSpec((per_step, count, width), lambda k, own: (k, 0, 0)),
        ),
    )(owners, *([grads] * per_step))


def reduce_scores(partial, ns, nl):
    w = partial.shape[0] // ns
    part = partial.reshape(ns, 1, w)
    out = pl.pallas_call(
        functools.partial(reduce_kernel, ns, nl),
        out_shape=jax.ShapeDtypeStruct((1, w), jnp.float32),
        in_specs=[pl.BlockSpec(memory_space=pltpu.VMEM)],
        out_specs=pl.BlockSpec(memory_space=pltpu.VMEM),
        scratch_shapes=[
            pltpu.VMEM((ns, 1, w), jnp.float32),
            pltpu.VMEM((1, w), jnp.float32),
            pltpu.VMEM((nl, 1, w), jnp.float32),
            pltpu.SemaphoreType.DMA((ns,)),
            pltpu.SemaphoreType.DMA((ns,)),
            pltpu.SemaphoreType.DMA((nl,)),
            pltpu.SemaphoreType.DMA((nl,)),
        ],
        compiler_params=pltpu.CompilerParams(collective_id=0, has_side_effects=True),
    )(part)
    return out.reshape(w)


def body(ns, nl, train_inputs, out_grads, query_blocks, basis_in, basis_out, block_of):
    acts = train_inputs[0]
    grads = out_grads[0]
    query = query_blocks[0]
    owners = block_of[0]
    count = acts.shape[0]
    rotated = turn_rows(acts, basis_in[0])
    width = grads.shape[1] // owners.shape[0]
    outgoing = pick_blocks(grads, owners)
    gathered, arrived = exchange(rotated, outgoing, ns)
    arrived = arrived.reshape(ns * count, width)
    rb = basis_out.shape[-1]
    turned = jnp.concatenate(
        [jnp.dot(arrived[:, e * rb:(e + 1) * rb], basis_out[0, e], preferred_element_type=jnp.float32) for e in range(basis_out.shape[1])],
        axis=1).astype(jnp.bfloat16)
    partial_scores = jnp.sum(
        lax.dot_general(
            gathered.reshape(ns * count, -1),
            query,
            (((1,), (1,)), ((), ())),
            preferred_element_type=jnp.float32,
        )
        * turned.astype(jnp.float32),
        axis=1,
    )
    return reduce_scores(partial_scores, ns, nl)


def solution(mesh):
    ns, nl = mesh.shape["seq"], mesh.shape["layer"]
    placed = (
        P("layer", "seq", None),
        P("layer", "seq", None),
        P("layer", "seq", None),
        P("layer", None, None, None),
        P("layer", "seq", None, None),
        P("layer", None),
    )
    return jax.shard_map(functools.partial(body, ns, nl), mesh=mesh, in_specs=placed, out_specs=P("seq"), check_vma=False)
```

profile of v0, /device:TPU:1, one launch (start us, length us, event | category | flops | bytes accessed | tf_op | source)
XLA Modules:
  0.0 289.6 jit_solution(2446649441258875766)
XLA Ops:
  0.0 0.0 copy-start
  0.0 1.5 copy.12
  1.6 0.0 copy-done
  1.6 0.9 convolution_convert_fusion.7
  2.4 1.4 copy.11.x_ref
  3.8 5.2 %shard_map.64.g_ref = bf16[16,128,896]{2,1,0:T(8,128)(2,1)} custom-call(s32[16]{0:T(128)} %bitcast.57, bf16[128,14336]{1,0:T(8,128)(2,1)} %bitcast.42, bf16[128,14336]{1,0:T(8,128)(2,1)} %bitcast.43, bf16[128,14336]{1,0:T(8,128)(2,1)} %bitcast.44, bf16[128,14336]{1,0:T(8,128)(2,1)} %bitcast.45), custom_call_target="tpu_custom_call" | custom-call | tf_op jit(solution)/shard_map/pallas_call | solution.py:238
  9.1 0.0 copy-start.1
  9.1 228.1 %shard_map.65 = (bf16[16,128,4096]{2,1,0:T(8,128)(2,1)}, bf16[16,128,896]{2,1,0:T(8,128)(2,1)}) custom-call(bf16[128,4096]{1,0:T(8,128)(2,1)} %copy.11.x_ref, bf16[16,128,896]{2,1,0:T(8,128)(2,1)} %shard_map.64.g_ref), custom_call_target="tpu_custom_call" | custom-call | tf_op jit(solution)/shard_map/pallas_call | solution.py:208
  237.2 0.0 copy-done.1
  237.2 1.4 fusion.10
  238.6 1.4 fusion.9
  240.0 1.4 fusion.8
  241.4 1.4 fusion.7
  242.7 1.4 fusion.6
  244.1 1.4 fusion.5
  245.5 1.4 fusion.4
  246.9 21.0 %multiply_reduce_fusion = f32[2048]{0:T(1024)} fusion(bf16[2048,896]{0,1:T(8,128)(2,1)S(1)} %fusion.4, bf16[2048,4096]{1,0:T(8,128)(2,1)} %bitcast.59, bf16[1,896,4096]{2,1,0:T(8,128)(2,1)} %param.8), kind=kOutput, calls=%fused_computation.2 | convolution fusion | flops 15037888512 | bytes 27795456 | tf_op jit(solution)/shard_map/dot_general | solution.py:288
  267.9 20.6 %shard_map.66 = f32[1,128]{1,0:T(1,128)} custom-call(f32[16,1,128]{2,1,0:T(1,128)} %bitcast.56), custom_call_target="tpu_custom_call" | custom-call | tf_op jit(solution)/shard_map/pallas_call | solution.py:253
  288.5 1.1 copy.22
Async XLA Ops:
  0.0 1.6 copy-start
  9.1 228.1 %copy-start.1 = (bf16[1,7,128,128]{3,2,1,0:T(8,128)(2,1)S(1)}, bf16[1,7,128,128]{3,2,1,0:T(8,128)(2,1)}, u32[]{:S(2)}) copy-start(bf16[1,7,128,128]{3,2,1,0:T(8,128)(2,1)} %param.10) | copy-start | bytes 688132
where the time goes:
time: 290 us
  Pallas kernels  254 us (88%)
  matrix products  31.5 us (11%)
  local copies, waits for them, and re-layouts  4.06 us (1%)
    pallas_call x1, Pallas kernels, exchange(): pl.pallas_call(functools.partial(comm_kernel, nx, nz, r1), out_shape=(jax...  228 us
    dot_general x1, matrix products, body(): lax.dot_general(gathered.reshape(ns * count, -1), query, (((1,), (1,)), (...  21 us
    pallas_call x1, Pallas kernels, reduce_scores(): pl.pallas_call(functools.partial(reduce_kernel, ns, nl), out_shape=jax.Sh...  20.6 us
    dot_general x7, matrix products, body(): jnp.dot(arrived[:, e * rb:(e + 1) * rb], basis_out[0, e], preferred_eleme...  9.67 us

commit v1 on v0

--- a/solution.py
+++ b/solution.py
@@ -143,14 +143,6 @@
             send(0, 0, 0, h, left)
         for e in offsets:
             send(0, 0, 0, None, at(e, 0), on_line(e))
-    gsends = []
-    for d in range(1, ns):
-        j = lax.rem(s + d, ns)
-        c = pltpu.make_async_remote_copy(
-            src_ref=g_ref.at[j], dst_ref=go_ref.at[s], send_sem=gssem.at[d - 1],
-            recv_sem=grsem.at[s], device_id=(j, lay), device_id_type=MESH)
-        c.start()
-        gsends.append(c)
     for e in offsets:
         cond = on_line(e)
         recv(e, 0, 1, None, cond)
@@ -176,6 +168,14 @@
         send(e, -1, 1, 0, right, cond)
         recv(e, 1, 1, 1, cond)
         send(e, 1, 1, 1, left, cond)
+    gsends = []
+    for d in range(1, ns):
+        j = lax.rem(s + d, ns)
+        c = pltpu.make_async_remote_copy(
+            src_ref=g_ref.at[j], dst_ref=go_ref.at[s], send_sem=gssem.at[d - 1],
+            recv_sem=grsem.at[s], device_id=(j, lay), device_id_type=MESH)
+        c.start()
+        gsends.append(c)
     if r1:
         for e in offsets:
             for dx in range(nx):

time: 290 us -> 291 us (level)
    pallas_call x1, Pallas kernels: 20.6 us -> 31.2 us  [reduce_scores(): pl.pallas_call(functools.partial(reduce_kernel, ns, nl), out_shape=jax.Sh...]
    pallas_call x1, Pallas kernels: 228 us -> 218 us  [exchange(): pl.pallas_call(functools.partial(comm_kernel, nx, nz, r1), out_shape=(jax...]
where the time goes in v1:
time: 291 us; the launch traced here: 290 us
  Pallas kernels  255 us (88%)
  matrix products  31.5 us (11%)
  local copies, waits for them, and re-layouts  4.06 us (1%)
    pallas_call x1, Pallas kernels, exchange(): pl.pallas_call(functools.partial(comm_kernel, nx, nz, r1), out_shape=(jax...  218 us
    pallas_call x1, Pallas kernels, reduce_scores(): pl.pallas_call(functools.partial(reduce_kernel, ns, nl), out_shape=jax.Sh...  31.2 us
    dot_general x1, matrix products, body(): lax.dot_general(gathered.reshape(ns * count, -1), query, (((1,), (1,)), (...  21 us
    dot_general x7, matrix products, body(): jnp.dot(arrived[:, e * rb:(e + 1) * rb], basis_out[0, e], preferred_eleme...  9.67 us

profile of v1, /device:TPU:1, one launch (start us, length us, event | category | flops | bytes accessed | tf_op | source)
XLA Modules:
  0.0 290.4 jit_solution(11351449859683602981)
XLA Ops:
  0.0 0.0 copy-start
  0.0 1.5 copy.12
  1.6 0.0 copy-done
  1.6 0.9 convolution_convert_fusion.7
  2.4 1.4 copy.11.x_ref
  3.8 5.2 %shard_map.64.g_ref = bf16[16,128,896]{2,1,0:T(8,128)(2,1)} custom-call(s32[16]{0:T(128)} %bitcast.57, bf16[128,14336]{1,0:T(8,128)(2,1)} %bitcast.42, bf16[128,14336]{1,0:T(8,128)(2,1)} %bitcast.43, bf16[128,14336]{1,0:T(8,128)(2,1)} %bitcast.44, bf16[128,14336]{1,0:T(8,128)(2,1)} %bitcast.45), custom_call_target="tpu_custom_call" | custom-call | tf_op jit(solution)/shard_map/pallas_call | solution.py:238
  9.1 0.0 copy-start.1
  9.1 218.3 %shard_map.65 = (bf16[16,128,4096]{2,1,0:T(8,128)(2,1)}, bf16[16,128,896]{2,1,0:T(8,128)(2,1)}) custom-call(bf16[128,4096]{1,0:T(8,128)(2,1)} %copy.11.x_ref, bf16[16,128,896]{2,1,0:T(8,128)(2,1)} %shard_map.64.g_ref), custom_call_target="tpu_custom_call" | custom-call | tf_op jit(solution)/shard_map/pallas_call | solution.py:208
  227.4 0.0 copy-done.1
  227.4 1.4 fusion.10
  228.8 1.4 fusion.9
  230.2 1.4 fusion.8
  231.6 1.4 fusion.7
  233.0 1.4 fusion.6
  234.4 1.4 fusion.5
  235.8 1.4 fusion.4
  237.2 21.0 %multiply_reduce_fusion = f32[2048]{0:T(1024)} fusion(bf16[2048,896]{0,1:T(8,128)(2,1)S(1)} %fusion.4, bf16[2048,4096]{1,0:T(8,128)(2,1)} %bitcast.59, bf16[1,896,4096]{2,1,0:T(8,128)(2,1)} %param.8), kind=kOutput, calls=%fused_computation.2 | convolution fusion | flops 15037888512 | bytes 27795456 | tf_op jit(solution)/shard_map/dot_general | solution.py:288
  258.1 31.2 %shard_map.66 = f32[1,128]{1,0:T(1,128)} custom-call(f32[16,1,128]{2,1,0:T(1,128)} %bitcast.56), custom_call_target="tpu_custom_call" | custom-call | tf_op jit(solution)/shard_map/pallas_call | solution.py:253
  289.3 1.1 copy.22
Async XLA Ops:
  0.0 1.6 copy-start
  9.1 218.4 %copy-start.1 = (bf16[1,7,128,128]{3,2,1,0:T(8,128)(2,1)S(1)}, bf16[1,7,128,128]{3,2,1,0:T(8,128)(2,1)}, u32[]{:S(2)}) copy-start(bf16[1,7,128,128]{3,2,1,0:T(8,128)(2,1)} %param.10) | copy-start | bytes 688132
